TPU v7x, 32 devices: a whole 2x2x4 slice. The times are simulated.
32 devices in a mesh: groups: 2 (over x), band: 8 (over z, y), sub: 2 (over core).
Axes of the slice: x: 2, y: 2, z: 4, core: 2. Of those that a mesh axis runs over, the one named last changes fastest.
Arguments:
- sky_maps: bfloat16 [32, 2, 32, 16384], P(('groups', 'band', 'sub')), parts along dimension 0, may hold values from -6 to 6
- sky_mask: float32 [32, 16384], P(('groups', 'band', 'sub')), parts along dimension 0, may hold values from 0.005 to 1, as said below
- pixel_counts: int32 [32], P(('groups', 'band', 'sub')), parts along dimension 0, may hold values from 8192 to 16384, as said below
- phi_offsets: int32 [32], P(('groups', 'band', 'sub')), parts along dimension 0, may hold values from 0 to 1
- low_orders: int32 [32], P('groups'), parts along dimension 0, may hold values from 1 to 4095, as said below
- legendre: bfloat16 [32, 8192, 32], P(('groups', 'band', 'sub')), parts along dimension 0, may hold values from -1 to 1
Outputs:
- alm_packed: float32 [32, 8192, 128], P(('groups', 'band', 'sub')), parts along dimension 0
- spectra: float32 [16384, 2, 1024], P(('groups', 'band', 'sub')), parts along dimension 0
There are 2 independent parts, one for each index of `groups`. A program takes and returns all parts, laid end to end along the dimension named above; each array names one. Nothing has to cross between parts.
Inputs may be any that keep to these rules, and one draw needn't show every extreme that they name: `pixel_counts`: multiples of 4; some cycle has exactly 16384 pixels; pixel slots at or past a cycle's count are not used. `low_orders`: all distinct. `sky_mask`: Positive.
All inputs are finite; a program needn't handle non-finite values.
Results may differ from a plain program's by a relative error of at most 0.0046.
Values may be sent and summed in bfloat16 or wider, within the bound.
A program may use at most 128 MiB of HBM per device.

v0:
```python
import jax
import jax.numpy as jnp
from jax import lax
from jax.sharding import PartitionSpec as P


def slot_orders(low_orders, degree_count):
    return jnp.stack([low_orders, degree_count - low_orders], axis=1).reshape(-1)


def finish_cycle(pixel_sums, cycle_count, orders):
    slots = orders.shape[0]
    maps_count = pixel_sums.shape[1] // 2
    inverse_root = 1.0 / jnp.sqrt(cycle_count.astype(jnp.float32))
    real_part = (pixel_sums[:slots] * inverse_root).reshape(slots, 2, maps_count)
    imag_part = (-pixel_sums[slots:] * inverse_root).reshape(slots, 2, maps_count)
    joined = jnp.stack(
        [real_part[:, 0], imag_part[:, 0], real_part[:, 1], imag_part[:, 1]], axis=1
    ).reshape(slots, 4 * maps_count)
    live_slots = 2 * orders < cycle_count
    return jnp.where(live_slots[:, None], joined, 0.0).astype(jnp.bfloat16)


def cycle_fourier(cycle_maps, cycle_mask, cycle_count, cycle_offset, orders):
    maps_count = cycle_maps.shape[1]
    pixel_slots = cycle_maps.shape[2]
    cycle_rows = cycle_maps.reshape(2 * maps_count, pixel_slots)
    block_width = min(2048, pixel_slots)
    group_count = block_width // 128
    slots = orders.shape[0]
    modulus = 2 * cycle_count
    scale = jnp.pi / cycle_count.astype(jnp.float32)
    order_mod = orders % modulus
    fine_units = 2 * order_mod[:, None] * jnp.arange(128, dtype=jnp.int32)[None, :] % modulus
    fine_angle = scale * fine_units.astype(jnp.float32)
    fine_cos = jnp.cos(fine_angle)[:, None, :]
    fine_sin = jnp.sin(fine_angle)[:, None, :]

    def add_block(block_index, totals):
        first_pixel = block_index * block_width
        row_block = lax.dynamic_slice_in_dim(cycle_rows, first_pixel, block_width, 1)
        mask_block = lax.dynamic_slice_in_dim(cycle_mask, first_pixel, block_width, 0)
        pixels = first_pixel + jnp.arange(block_width, dtype=jnp.int32)
        masked = jnp.where(
            pixels[None, :] < cycle_count, mask_block[None, :] * row_block.astype(jnp.float32), 0.0
        ).astype(jnp.bfloat16)
        group_starts = first_pixel + 128 * jnp.arange(group_count, dtype=jnp.int32)
        coarse_units = (
            order_mod[:, None] * ((2 * group_starts[None, :] + cycle_offset) % modulus) % modulus
        )
        coarse_angle = scale * coarse_units.astype(jnp.float32)
        coarse_cos = jnp.cos(coarse_angle)[:, :, None]
        coarse_sin = jnp.sin(coarse_angle)[:, :, None]
        cosines = (coarse_cos * fine_cos - coarse_sin * fine_sin).reshape(slots, block_width)
        sines = (coarse_sin * fine_cos + coarse_cos * fine_sin).reshape(slots, block_width)
        tables = jnp.concatenate([cosines.astype(jnp.bfloat16), sines.astype(jnp.bfloat16)], axis=0)
        return totals + lax.dot_general(
            tables, masked, (((1,), (1,)), ((), ())), preferred_element_type=jnp.float32
        )

    block_count = (cycle_count + block_width - 1) // block_width
    pixel_sums = lax.fori_loop(
        0, block_count, add_block, jnp.zeros((2 * slots, 2 * maps_count), jnp.float32)
    )
    return finish_cycle(pixel_sums, cycle_count, orders)


def stacked_operand(block_rows):
    quarter = block_rows.shape[1] // 4
    q_real = block_rows[:, :quarter]
    q_imag = block_rows[:, quarter : 2 * quarter]
    u_real = block_rows[:, 2 * quarter : 3 * quarter]
    u_imag = block_rows[:, 3 * quarter :]
    lower_half = jnp.concatenate([u_imag, -u_real, -q_imag, q_real], axis=1)
    return jnp.concatenate([block_rows, lower_half], axis=0)


def pair_alm(legendre_rows, first_order, first_block, second_block):
    first_operand = stacked_operand(first_block)
    second_operand = stacked_operand(second_block)
    degree_count, inner_width = legendre_rows.shape
    tile_height = min(128, degree_count)
    tile_count = degree_count // tile_height
    split_row = degree_count - first_order
    tile_starts = jnp.arange(tile_count, dtype=jnp.int32) * tile_height
    chosen = jnp.where(
        (tile_starts < split_row)[:, None, None], first_operand[None], second_operand[None]
    )
    tile_product = jnp.einsum(
        "tir,tro->tio",
        legendre_rows.reshape(tile_count, tile_height, inner_width),
        chosen,
        preferred_element_type=jnp.float32,
    )
    tile_product = tile_product.reshape(degree_count, first_operand.shape[1])
    border = split_row // tile_height * tile_height
    border_rows = lax.dynamic_slice_in_dim(legendre_rows, border, tile_height, 0)
    border_product = jnp.dot(border_rows, second_operand, preferred_element_type=jnp.float32)
    current = lax.dynamic_slice_in_dim(tile_product, border, tile_height, 0)
    row_index = border + jnp.arange(tile_height, dtype=jnp.int32)
    patched = jnp.where((row_index >= split_row)[:, None], border_product, current)
    return -lax.dynamic_update_slice_in_dim(tile_product, patched, border, 0)


def dense_pair(alm_rows, first_order):
    degree_count = alm_rows.shape[0]
    degrees = jnp.arange(degree_count, dtype=jnp.int32)
    first_dense = jnp.where(
        (degrees >= first_order)[:, None], jnp.roll(alm_rows, first_order, axis=0), 0.0
    ).astype(jnp.bfloat16)
    second_dense = jnp.where(
        (degrees >= degree_count - first_order)[:, None], alm_rows, 0.0
    ).astype(jnp.bfloat16)
    return jnp.stack([first_dense, second_dense], axis=0)


def outer_totals(rows, maps_count):
    split_parts = rows.reshape(rows.shape[0], rows.shape[1], 2, 2, maps_count)
    return jnp.einsum(
        "slerm,slern->lemn", split_parts, split_parts, preferred_element_type=jnp.float32
    )


def scaled_spectra(totals, degrees, orders, weight, maps_count):
    counts = jnp.maximum(
        jnp.sum((orders[None, :] <= degrees[:, None]).astype(jnp.int32), axis=1), 1
    ).astype(jnp.float32)
    return (2.0 * totals / (weight * counts)[:, None, None, None]).reshape(
        degrees.shape[0], 2, maps_count * maps_count
    )


def local(sky_maps, sky_mask, pixel_counts, phi_offsets, low_orders, legendre):
    devices = lax.axis_size(("band", "sub"))
    device_index = lax.axis_index(("band", "sub"))
    degree_count = legendre.shape[1]
    orders = slot_orders(low_orders, degree_count)
    cycle_local = sky_maps.shape[0]
    maps_count = sky_maps.shape[2]
    pair_local = legendre.shape[0]
    slot_local = 2 * pair_local
    columns = 4 * maps_count
    valid_pixels = jnp.arange(sky_maps.shape[3], dtype=jnp.int32)[None, :] < pixel_counts[:, None]
    local_square = jnp.sum(jnp.where(valid_pixels, sky_mask * sky_mask, 0.0))
    local_pixels = jnp.sum(pixel_counts.astype(jnp.float32))
    total_square, total_pixels = lax.psum((local_square, local_pixels), ("band", "sub"))
    weight = total_square / total_pixels
    cycle_blocks = [
        cycle_fourier(sky_maps[0], sky_mask[0], pixel_counts[0], phi_offsets[0], orders)
    ]
    coefficients = jnp.stack(cycle_blocks, axis=1).reshape(
        devices, slot_local, cycle_local, columns
    )
    received = lax.all_to_all(
        coefficients, ("band", "sub"), split_axis=0, concat_axis=0, tiled=True
    )
    cycle_total = devices * cycle_local
    first_order = lax.dynamic_index_in_dim(
        low_orders, device_index * pair_local + 0, 0, keepdims=False
    )
    first_block = received[:, 0].reshape(cycle_total, columns)
    second_block = received[:, 1].reshape(cycle_total, columns)
    alm_pairs = [pair_alm(legendre[0], first_order, first_block, second_block)]
    alm_packed = jnp.stack(alm_pairs, axis=0)
    dense_local = dense_pair(alm_pairs[0], first_order)
    by_degree = lax.all_to_all(
        dense_local, ("band", "sub"), split_axis=1, concat_axis=0, tiled=True
    )
    degree_local = by_degree.shape[1]
    degrees = device_index * degree_local + jnp.arange(degree_local, dtype=jnp.int32)
    totals = outer_totals(by_degree, maps_count)
    spectra = scaled_spectra(totals, degrees, orders, weight, maps_count)
    return (alm_packed, spectra)


def solution(mesh):
    placed = (
        P(("groups", "band", "sub"), None, None, None),
        P(("groups", "band", "sub"), None),
        P(("groups", "band", "sub")),
        P(("groups", "band", "sub")),
        P("groups"),
        P(("groups", "band", "sub"), None, None),
    )
    return jax.shard_map(
        local,
        mesh=mesh,
        in_specs=placed,
        out_specs=(
            P(("groups", "band", "sub"), None, None),
            P(("groups", "band", "sub"), None, None),
        ),
        check_vma=False,
    )
```

profile of v0, /device:TPU:18, one launch (start us, length us, event | category | flops | bytes accessed | tf_op | source)
XLA Modules:
  0.0 302.1 jit_solution(14685588854479680032)
XLA Ops:
  1.4 0.7 subtract_bitcast_fusion
  2.0 0.7 pad_add_fusion
  3.1 34.6 %while.14 = (s32[]{:T(128)}, f32[64,64]{1,0:T(8,128)S(1)}, s32[]{:T(128)}, f32[]{:T(128)}, s32[32]{0:T(128)S(1)}, /*index=5*/s32[]{:T(128)}, s32[]{:T(128)}, pre...) while((s32[]{:T(128)}, f32[64,64]{1,0:T(8,128)S(1)}, ...), condition=%wide.region_1.2_spmd.clone.clone, body=%wide.region_0.1_spmd.clone.clone.sunk | while | flops 18404532 | bytes 1446522 | solution.py:62
  3.4 0.8 and_select_fusion.4
  4.8 0.7 dynamic_slice.63
  5.5 0.7 add_compare_fusion.3
  6.2 1.2 convolution_add_fusion.2
  7.8 0.8 and_select_fusion.4
  9.2 0.7 dynamic_slice.63
  10.5 1.2 convolution_add_fusion.2
  12.1 0.8 and_select_fusion.4
  13.5 0.7 dynamic_slice.63
  14.2 0.7 add_compare_fusion.3
  14.9 1.2 convolution_add_fusion.2
  16.4 0.8 and_select_fusion.4
  17.8 0.7 dynamic_slice.63
  18.5 0.7 add_compare_fusion.3
  19.2 1.2 convolution_add_fusion.2
  20.8 0.8 and_select_fusion.4
  22.2 0.7 dynamic_slice.63
  23.5 1.2 convolution_add_fusion.2
  25.1 0.8 and_select_fusion.4
  26.5 0.7 dynamic_slice.63
  27.2 0.7 add_compare_fusion.3
  27.9 1.2 convolution_add_fusion.2
  29.4 0.8 and_select_fusion.4
  30.8 0.7 dynamic_slice.63
  32.2 1.2 convolution_add_fusion.2
  33.7 0.8 and_select_fusion.4
  35.2 0.7 dynamic_slice.63
  36.5 1.2 convolution_add_fusion.2
  38.3 0.7 select_convert_fusion.3
  38.9 5.6 %all-to-all-start = ((bf16[16,2,1,128]{3,1,2,0:T(2,128)(2,1)}), bf16[16,2,1,128]{3,1,2,0:T(2,128)(2,1)S(1)}, u32[]{:S(2)}, u32[]{:S(2)}) async-start(bf16[16,2,1,128]{3,1,2,0:T(2,128)(2,1)} %select_convert_fusion.3), calls=%async_computation | async-start | bytes 16384 | tf_op jit(solution)/shard_map/all_to_all | solution.py:154
  45.8 0.7 iota_compare_fusion.1
  49.0 0.9 fusion.34
  50.3 5.4 %fusion.31 = (bf16[1,8192,128]{2,1,0:T(8,128)(2,1)S(1)}, f32[1,8192,128]{2,1,0:T(8,128)}) fusion(pred[8192]{0:T(1024)(128)(4,1)S(1)} %iota_compare_fusion, f32[8192,128]{1,0:T(8,128)S(1)} %fusion.33), kind=kLoop, calls=%fused_computation.49 | loop fusion | flops 3145728 | bytes 10493952 | tf_op jit(solution)/shard_map/stack | solution.py:114
  55.7 11.8 %fusion.32 = bf16[1,8192,128]{2,1,0:T(8,128)(2,1)S(1)} fusion(s32[]{:T(128)S(6)} %select_n.144, bf16[8192,128]{1,0:T(8,128)(2,1)S(1)} %neg.23, pred[8192]{0:T(1024)(128)(4,1)S(1)} %iota_compare_fusion.1), kind=kLoop, calls=%fused_computation.50 | loop fusion | flops 5242880 | bytes 4202500 | tf_op jit(solution)/shard_map/stack | solution.py:114
  67.9 35.4 %copy.69 = bf16[2,8192,128]{2,0,1:T(2,128)(2,1)} copy(bf16[2,8192,128]{2,1,0:T(8,128)(2,1)S(1)} %pad_maximum_fusion) | data formatting | bytes 8388608 | tf_op jit(solution)/shard_map/stack | solution.py:114
  103.3 6.8 %all-to-all-start.1 = ((bf16[2,8192,128]{2,0,1:T(2,128)(2,1)}), bf16[2,8192,128]{2,0,1:T(2,128)(2,1)}, u32[]{:S(2)}, u32[]{:S(2)}) async-start(bf16[2,8192,128]{2,0,1:T(2,128)(2,1)} %copy.69), calls=%async_computation.1 | async-start | bytes 8388608 | tf_op jit(solution)/shard_map/all_to_all | solution.py:166
  110.2 0.8 fusion.40
  111.0 110.5 %all-reduce = (f32[]{:T(128)}, f32[]{:T(128)}) all-reduce(f32[]{:T(128)} %fusion.40, f32[]{:T(128)} %bitcast.21), channel_id=1, replica_groups=mesh['groups'=2,'band'=8,'sub'=2] {'band','sub'}, use_global_device_ids=true, to_apply=%region_3.4 | all-reduce | flops 2 | bytes 16 | tf_op jit(solution)/shard_map/psum | solution.py:146
  222.9 4.7 %copy.70 = bf16[2,8192,128]{2,1,0:T(8,128)(2,1)} copy(bf16[2,8192,128]{2,0,1:T(2,128)(2,1)} %all-to-all-done.1) | data formatting | bytes 8388608 | tf_op jit(solution)/shard_map/all_to_all | solution.py:166
  227.6 6.4 %copy.71 = bf16[16,2,512,128]{2,3,1,0:T(8,128)(2,1)} copy(bf16[16,2,512,128]{3,2,0,1:T(8,128)(2,1)} %bitcast.69) | data formatting | bytes 8388608 | tf_op jit(solution)/shard_map/all_to_all | solution.py:166
  234.1 23.2 %copy.73 = bf16[32,512,2,2,32]{4,0,3,2,1:T(8,128)(2,1)} copy(bf16[32,512,2,2,32]{1,4,3,2,0:T(8,128)(2,1)} %bitcast.67) | data formatting | bytes 8388608 | tf_op jit(solution)/shard_map/reshape | solution.py:118
  257.3 21.0 %convolution_bitcast_fusion = f32[512,2,32,32]{3,2,1,0:T(8,128)} fusion(bf16[32,512,2,2,32]{4,0,3,2,1:T(8,128)(2,1)} %copy.73), kind=kOutput, calls=%fused_computation.40 | convolution fusion | flops 134217728 | bytes 8388608 | tf_op jit(solution)/shard_map/slerm,slern->lemn/dot_general | solution.py:119
  278.3 11.4 %copy.74 = f32[512,2,32,32]{0,3,2,1:T(8,128)} copy(f32[512,2,32,32]{3,2,1,0:T(8,128)} %convolution_bitcast_fusion) | data formatting | bytes 8388608 | tf_op jit(solution)/shard_map/slerm,slern->lemn/dot_general | solution.py:119
  289.7 5.1 %multiply_divide_fusion = f32[512,2,32,32]{0,3,2,1:T(8,128)} fusion(f32[512,2,32,32]{0,3,2,1:T(8,128)} %copy.74, f32[512]{0:T(512)S(1)} %convert_multiply_fusion), kind=kLoop, calls=%fused_computation.47 | loop fusion | flops 2097152 | bytes 8390656 | tf_op jit(solution)/shard_map/div | solution.py:128
  294.8 7.3 %copy.75 = f32[512,2,1024]{2,1,0:T(2,128)} copy(f32[512,2,1024]{0,2,1:T(8,128)} %bitcast.68) | data formatting | bytes 8388608
  (74 shorter events, 13.2 us)
Async XLA Ops:
  3.0 35.1 %copy-start.2 = (s32[16]{0:T(128)S(1)}, s32[16]{0:T(128)}, u32[]{:S(2)}) copy-start(s32[16]{0:T(128)} %param.12) | copy-start | bytes 196
  3.0 45.5 %copy-start = (bf16[1,8192,32]{1,2,0:T(8,128)(2,1)S(1)}, bf16[1,8192,32]{1,2,0:T(8,128)(2,1)}, u32[]{:S(2)}) copy-start(bf16[1,8192,32]{1,2,0:T(8,128)(2,1)} %param.13) | copy-start | bytes 1572868
  38.9 9.7 %all-to-all-start = ((bf16[16,2,1,128]{3,1,2,0:T(2,128)(2,1)}), bf16[16,2,1,128]{3,1,2,0:T(2,128)(2,1)S(1)}, u32[]{:S(2)}, u32[]{:S(2)}) async-start(bf16[16,2,1,128]{3,1,2,0:T(2,128)(2,1)} %select_convert_fusion.3), calls=%async_computation | async-start | bytes 16384 | tf_op jit(solution)/shard_map/all_to_all | solution.py:154
  103.3 6.8 %copy-start.1 = (f32[16384]{0:T(1024)S(1)}, f32[16384]{0:T(1024)}, u32[]{:S(2)}) copy-start(f32[16384]{0:T(1024)} %get-tuple-element.441) | copy-start | bytes 196612
  103.3 119.5 %all-to-all-start.1 = ((bf16[2,8192,128]{2,0,1:T(2,128)(2,1)}), bf16[2,8192,128]{2,0,1:T(2,128)(2,1)}, u32[]{:S(2)}, u32[]{:S(2)}) async-start(bf16[2,8192,128]{2,0,1:T(2,128)(2,1)} %copy.69), calls=%async_computation.1 | async-start | bytes 8388608 | tf_op jit(solution)/shard_map/all_to_all | solution.py:166
where the time goes:
time: 304 us; the launch traced here: 302 us
  blocking collectives  111 us (37%)
  local copies, waits for them, and re-layouts  95.9 us (32%)
  other arithmetic  45.7 us (15%)
  matrix products  31.5 us (10%)
  starting transfers between devices  12.4 us (4%)
  between operations  5.55 us (2%)
    psum x1, blocking collectives, local(): lax.psum((local_square, local_pixels), ('band', 'sub'))  111 us
    another operation x1, local copies, waits for them, and re-layouts, dense_pair(): return jnp.stack([first_dense, second_dense], axis=0)  35.4 us
    reshape x1, local copies, waits for them, and re-layouts, outer_totals(): split_parts = rows.reshape(rows.shape[0], rows.shape[1], 2, 2, maps_count)  23.2 us
    dot_general x1, matrix products, outer_totals(): jnp.einsum('slerm,slern->lemn', split_parts, split_parts, preferred_eleme...  21 us
    another operation x3, other arithmetic, dense_pair(): return jnp.stack([first_dense, second_dense], axis=0)  17.6 us
    dot_general x1, local copies, waits for them, and re-layouts, outer_totals(): jnp.einsum('slerm,slern->lemn', split_parts, split_parts, preferred_eleme...  11.4 us
    all_to_all x2, local copies, waits for them, and re-layouts, local(): lax.all_to_all(dense_local, ('band', 'sub'), split_axis=1, concat_axis=0,...  11.2 us
    dot_general x8, matrix products, add_block(): lax.dot_general(tables, masked, (((1,), (1,)), ((), ())), preferred_eleme...  9.41 us
  transfers between devices with their start and end apart: 2, of which 0 were waited for; matrix products, arithmetic and copies ran while one was open for 1% of the time, Pallas kernels for 0%

commit v1 on v0

--- a/solution.py
+++ b/solution.py
@@ -163,9 +163,9 @@
     alm_pairs = [pair_alm(legendre[0], first_order, first_block, second_block)]
     alm_packed = jnp.stack(alm_pairs, axis=0)
     dense_local = dense_pair(alm_pairs[0], first_order)
-    by_degree = lax.all_to_all(
-        dense_local, ("band", "sub"), split_axis=1, concat_axis=0, tiled=True
-    )
+    cells = jnp.split(dense_local, lax.axis_size(("band", "sub")), axis=1)
+    got = lax.all_to_all(jnp.stack(cells), ("band", "sub"), 0, 0)
+    by_degree = jnp.concatenate(got, axis=0)
     degree_local = by_degree.shape[1]
     degrees = device_index * degree_local + jnp.arange(degree_local, dtype=jnp.int32)
     totals = outer_totals(by_degree, maps_count)

time: 304 us -> 275 us (0.905)
  local copies, waits for them, and re-layouts: 95.9 us -> 55.7 us
  other arithmetic: 45.7 us -> 56.9 us
    reshape x1 -> x0, local copies, waits for them, and re-layouts: 23.2 us -> none  [outer_totals(): split_parts = rows.reshape(rows.shape[0], rows.shape[1], 2, 2, maps_count)]
    another operation x1, local copies, waits for them, and re-layouts: 35.4 us -> 23.2 us  [outer_totals(): split_parts = rows.reshape(rows.shape[0], rows.shape[1], 2, 2, maps_count)]
    unnamed x0 -> x15, other arithmetic: none -> 10.8 us
    all_to_all x2 -> x1, local copies, waits for them, and re-layouts: 11.2 us -> 6.4 us  [local(): got = lax.all_to_all(jnp.stack(cells), ('band', 'sub'), 0, 0)]
    another operation x3 -> x2, other arithmetic: 17.6 us -> 17.2 us  [dense_pair(): return jnp.stack([first_dense, second_dense], axis=0)]
where the time goes in v1:
time: 275 us; the launch traced here: 273 us
  blocking collectives  111 us (40%)
  other arithmetic  56.9 us (21%)
  local copies, waits for them, and re-layouts  55.7 us (20%)
  matrix products  31.5 us (11%)
  starting transfers between devices  12.4 us (5%)
  between operations  5.55 us (2%)
    psum x1, blocking collectives, local(): lax.psum((local_square, local_pixels), ('band', 'sub'))  111 us
    another operation x1, local copies, waits for them, and re-layouts, outer_totals(): split_parts = rows.reshape(rows.shape[0], rows.shape[1], 2, 2, maps_count)  23.2 us
    dot_general x1, matrix products, outer_totals(): jnp.einsum('slerm,slern->lemn', split_parts, split_parts, preferred_eleme...  21 us
    another operation x2, other arithmetic, dense_pair(): return jnp.stack([first_dense, second_dense], axis=0)  17.2 us
    dot_general x1, local copies, waits for them, and re-layouts, outer_totals(): jnp.einsum('slerm,slern->lemn', split_parts, split_parts, preferred_eleme...  11.4 us
    unnamed x15, other arithmetic  10.8 us
    dot_general x8, matrix products, add_block(): lax.dot_general(tables, masked, (((1,), (1,)), ((), ())), preferred_eleme...  9.41 us
    unnamed x10, local copies, waits for them, and re-layouts  7.43 us
  transfers between devices with their start and end apart: 2, of which 0 were waited for; matrix products, arithmetic and copies ran while one was open for 1% of the time, Pallas kernels for 0%

profile of v1, /device:TPU:18, one launch (start us, length us, event | category | flops | bytes accessed | tf_op | source)
XLA Modules:
  0.0 273.0 jit_solution(2661794675630945643)
XLA Ops:
  3.1 34.6 %while.14 = (s32[]{:T(128)}, f32[64,64]{1,0:T(8,128)S(1)}, s32[]{:T(128)}, f32[]{:T(128)}, s32[32]{0:T(128)S(1)}, /*index=5*/s32[]{:T(128)}, s32[]{:T(128)}, pre...) while((s32[]{:T(128)}, f32[64,64]{1,0:T(8,128)S(1)}, ...), condition=%wide.region_1.2_spmd.clone.clone, body=%wide.region_0.1_spmd.clone.clone.sunk | while | flops 18404532 | bytes 1446522 | solution.py:62
  3.4 0.8 and_select_fusion.4
  4.8 0.7 dynamic_slice.63
  6.2 1.2 convolution_add_fusion.2
  7.8 0.8 and_select_fusion.4
  10.5 1.2 convolution_add_fusion.2
  12.1 0.8 and_select_fusion.4
  13.5 0.7 dynamic_slice.63
  14.9 1.2 convolution_add_fusion.2
  16.4 0.8 and_select_fusion.4
  19.2 1.2 convolution_add_fusion.2
  20.8 0.8 and_select_fusion.4
  23.5 1.2 convolution_add_fusion.2
  25.1 0.8 and_select_fusion.4
  27.9 1.2 convolution_add_fusion.2
  29.4 0.8 and_select_fusion.4
  32.2 1.2 convolution_add_fusion.2
  33.7 0.8 and_select_fusion.4
  36.5 1.2 convolution_add_fusion.2
  38.9 5.6 %all-to-all-start = ((bf16[16,2,1,128]{3,1,2,0:T(2,128)(2,1)}), bf16[16,2,1,128]{3,1,2,0:T(2,128)(2,1)S(1)}, u32[]{:S(2)}, u32[]{:S(2)}) async-start(bf16[16,2,1,128]{3,1,2,0:T(2,128)(2,1)} %select_convert_fusion.3), calls=%async_computation | async-start | bytes 16384 | tf_op jit(solution)/shard_map/all_to_all | solution.py:154
  49.0 0.9 fusion.34
  50.3 5.4 %fusion.31 = (bf16[1,8192,128]{2,1,0:T(8,128)(2,1)S(1)}, f32[1,8192,128]{2,1,0:T(8,128)}) fusion(pred[8192]{0:T(1024)(128)(4,1)S(1)} %iota_compare_fusion, f32[8192,128]{1,0:T(8,128)S(1)} %fusion.33), kind=kLoop, calls=%fused_computation.78 | loop fusion | flops 3145728 | bytes 10493952 | tf_op jit(solution)/shard_map/stack | solution.py:114
  55.7 11.8 %fusion.32 = bf16[1,8192,128]{2,1,0:T(8,128)(2,1)S(1)} fusion(s32[]{:T(128)S(6)} %select_n.144, bf16[8192,128]{1,0:T(8,128)(2,1)S(1)} %neg.23, pred[8192]{0:T(1024)(128)(4,1)S(1)} %iota_compare_fusion.1), kind=kLoop, calls=%fused_computation.79 | loop fusion | flops 5242880 | bytes 4202500 | tf_op jit(solution)/shard_map/stack | solution.py:114
  67.5 0.7 bitcast_dynamic-update-slice_fusion.14
  68.2 0.7 bitcast_dynamic-update-slice_fusion.13
  69.0 0.7 bitcast_dynamic-update-slice_fusion.12
  69.7 0.7 bitcast_dynamic-update-slice_fusion.11
  70.4 0.7 bitcast_dynamic-update-slice_fusion.10
  71.1 0.7 bitcast_dynamic-update-slice_fusion.9
  71.8 0.7 bitcast_dynamic-update-slice_fusion.8
  72.6 0.7 bitcast_dynamic-update-slice_fusion.7
  73.3 0.7 bitcast_dynamic-update-slice_fusion.6
  74.0 0.7 bitcast_dynamic-update-slice_fusion.5
  74.7 0.7 bitcast_dynamic-update-slice_fusion.4
  75.4 0.7 bitcast_dynamic-update-slice_fusion.3
  76.2 0.7 bitcast_dynamic-update-slice_fusion.2
  76.9 0.7 bitcast_dynamic-update-slice_fusion.1
  77.6 0.7 bitcast_dynamic-update-slice_fusion
  78.3 0.7 fusion.54
  79.0 6.8 %all-to-all-start.1 = ((bf16[16,2,512,128]{3,2,1,0:T(8,128)(2,1)}), bf16[16,2,512,128]{3,2,1,0:T(8,128)(2,1)}, u32[]{:S(2)}, u32[]{:S(2)}) async-start(bf16[16,2,512,128]{3,2,1,0:T(8,128)(2,1)} %fusion.54), calls=%async_computation.1 | async-start | bytes 8388608 | tf_op jit(solution)/shard_map/all_to_all | solution.py:167
  85.9 0.8 fusion.57
  86.7 110.5 %all-reduce = (f32[]{:T(128)}, f32[]{:T(128)}) all-reduce(f32[]{:T(128)} %fusion.57, f32[]{:T(128)} %bitcast.35), channel_id=1, replica_groups=mesh['groups'=2,'band'=8,'sub'=2] {'band','sub'}, use_global_device_ids=true, to_apply=%region_3.4 | all-reduce | flops 2 | bytes 16 | tf_op jit(solution)/shard_map/psum | solution.py:146
  198.6 6.4 %copy.64 = bf16[16,2,512,128]{2,3,1,0:T(8,128)(2,1)} copy(bf16[16,2,512,128]{3,2,1,0:T(8,128)(2,1)} %all-to-all-done.1) | data formatting | bytes 8388608 | tf_op jit(solution)/shard_map/all_to_all | solution.py:167
  205.0 23.2 %copy.66 = bf16[32,512,2,2,32]{4,0,3,2,1:T(8,128)(2,1)} copy(bf16[32,512,2,2,32]{1,4,3,2,0:T(8,128)(2,1)} %bitcast.98) | data formatting | bytes 8388608 | tf_op jit(solution)/shard_map/reshape;reshape | solution.py:118
  228.2 21.0 %convolution_bitcast_fusion = f32[512,2,32,32]{3,2,1,0:T(8,128)} fusion(bf16[32,512,2,2,32]{4,0,3,2,1:T(8,128)(2,1)} %copy.66), kind=kOutput, calls=%fused_computation.70 | convolution fusion | flops 134217728 | bytes 8388608 | tf_op jit(solution)/shard_map/slerm,slern->lemn/dot_general | solution.py:119
  249.3 11.4 %copy.67 = f32[512,2,32,32]{0,3,2,1:T(8,128)} copy(f32[512,2,32,32]{3,2,1,0:T(8,128)} %convolution_bitcast_fusion) | data formatting | bytes 8388608 | tf_op jit(solution)/shard_map/slerm,slern->lemn/dot_general | solution.py:119
  260.7 5.1 %multiply_divide_fusion = f32[512,2,32,32]{0,3,2,1:T(8,128)} fusion(f32[512,2,32,32]{0,3,2,1:T(8,128)} %copy.67, f32[512]{0:T(512)S(1)} %convert_multiply_fusion), kind=kLoop, calls=%fused_computation.76 | loop fusion | flops 2097152 | bytes 8390656 | tf_op jit(solution)/shard_map/div | solution.py:128
  265.7 7.3 %copy.68 = f32[512,2,1024]{2,1,0:T(2,128)} copy(f32[512,2,1024]{0,2,1:T(8,128)} %bitcast.99) | data formatting | bytes 8388608
  (87 shorter events, 22.3 us)
Async XLA Ops:
  3.0 35.1 %copy-start.2 = (s32[16]{0:T(128)S(1)}, s32[16]{0:T(128)}, u32[]{:S(2)}) copy-start(s32[16]{0:T(128)} %param.12) | copy-start | bytes 196
  3.0 45.5 %copy-start = (bf16[1,8192,32]{1,2,0:T(8,128)(2,1)S(1)}, bf16[1,8192,32]{1,2,0:T(8,128)(2,1)}, u32[]{:S(2)}) copy-start(bf16[1,8192,32]{1,2,0:T(8,128)(2,1)} %param.13) | copy-start | bytes 1572868
  38.9 9.7 %all-to-all-start = ((bf16[16,2,1,128]{3,1,2,0:T(2,128)(2,1)}), bf16[16,2,1,128]{3,1,2,0:T(2,128)(2,1)S(1)}, u32[]{:S(2)}, u32[]{:S(2)}) async-start(bf16[16,2,1,128]{3,1,2,0:T(2,128)(2,1)} %select_convert_fusion.3), calls=%async_computation | async-start | bytes 16384 | tf_op jit(solution)/shard_map/all_to_all | solution.py:154
  79.0 6.8 %copy-start.1 = (f32[16384]{0:T(1024)S(1)}, f32[16384]{0:T(1024)}, u32[]{:S(2)}) copy-start(f32[16384]{0:T(1024)} %get-tuple-element.439) | copy-start | bytes 196612
  79.0 119.5 %all-to-all-start.1 = ((bf16[16,2,512,128]{3,2,1,0:T(8,128)(2,1)}), bf16[16,2,512,128]{3,2,1,0:T(8,128)(2,1)}, u32[]{:S(2)}, u32[]{:S(2)}) async-start(bf16[16,2,512,128]{3,2,1,0:T(8,128)(2,1)} %fusion.54), calls=%async_computation.1 | async-start | bytes 8388608 | tf_op jit(solution)/shard_map/all_to_all | solution.py:167
